TPU v7x, 512 devices: a whole 4x4x16 slice. The times are simulated.
512 devices in a mesh: dp: 16 (over z_hi, x), shard: 32 (over y, z_lo, core).
Axes of the slice: x: 4, y: 4, z: 16 (z_hi: 4, z_lo: 4; z = z_hi * 4 + z_lo), core: 2. Of those that a mesh axis runs over, the one named last changes fastest.
Arguments:
- inputs: bfloat16 [2, 4096, 8192], P(None, 'dp', 'shard'), may hold values from -6 to 6
- key_panel: bfloat16 [8192, 4096], P('dp', 'shard'), may hold values from -0.0625 to 0.0625
- value_panel: bfloat16 [8192, 4096], P('dp', 'shard'), may hold values from -0.0625 to 0.0625
- short_filters: float32 [2, 4096, 7], P(None, 'shard'), may hold values from -2 to 2
- medium_filters: float32 [256, 128], P('shard'), may hold values from -0.5 to 0.5
- lengths: int32 [2], replicated, may hold values from 2048 to 4096, as said below
- cotangent: bfloat16 [2, 4096, 4096], P(None, 'dp', 'shard'), may hold values from -0.099609375 to 0.099609375
Outputs:
- mixed: bfloat16 [2, 4096, 4096], P(None, 'dp', 'shard')
- key_grad: bfloat16 [8192, 4096], P('dp', 'shard')
- value_grad: bfloat16 [8192, 4096], P('dp', 'shard')
- short_grad: float32 [2, 4096, 7], P(None, 'shard')
- medium_grad: float32 [256, 128], P('shard')
Inputs may be any that keep to these rules, and one draw needn't show every extreme that they name: `lengths`: each length is a multiple of 16; one window in every draw has the full length 4096, the others are shorter.
All inputs are finite; a program needn't handle non-finite values.
Results may differ from a plain program's by a relative error of at most 0.014.
Values may be sent and summed in bfloat16 or wider, within the bound.
No kernel may reach another device: no remote copies, remote signals or barrier semaphores. Data moves between devices by JAX's collectives and lax.ppermute only.
A program may use at most 64 MiB of HBM per device.

v0:
```python
import jax
import jax.numpy as jnp
from jax import lax
from jax.sharding import PartitionSpec as P


def shifted(value, axis, steps):
    count = lax.axis_size(axis)
    first, last = (max(0, -steps), min(count, count - steps))
    return lax.ppermute(value, axis, [(source, source + steps) for source in range(first, last)])


def band(filters, count):
    groups, taps = filters.shape
    width = count + taps - 1
    padded = jnp.concatenate([filters, jnp.zeros((groups, count), jnp.float32)], axis=1)
    tiled = jnp.tile(padded, (1, count))[:, : count * width]
    return tiled.reshape(groups, count, width)


def band_sums(correlation, count, taps):
    groups, _, width = correlation.shape
    flat = correlation.reshape(groups, count * width)
    padded = jnp.concatenate([flat, jnp.zeros((groups, count), jnp.float32)], axis=1)
    skewed = padded.reshape(groups, count, width + 1)
    return jnp.sum(skewed, axis=1)[:, :taps][:, ::-1]


def short_taps(extended, filters, count):
    width = filters.shape[-1]
    total = jnp.zeros(extended.shape[:2] + (count, extended.shape[3]), jnp.float32)
    for tap in range(width):
        begin = width - 1 - tap
        total = total + filters[:, None, None, :, tap] * extended[
            :, :, begin : begin + count
        ].astype(jnp.float32)
    return total


def short_ahead(extended, filters, count):
    width = filters.shape[-1]
    total = jnp.zeros(extended.shape[:2] + (count, extended.shape[3]), jnp.float32)
    for tap in range(width):
        total = total + filters[:, None, None, :, tap] * extended[:, :, tap : tap + count]
    return total


def filter_terms(grads, extended, count, width):
    columns = []
    for tap in range(width):
        begin = width - 1 - tap
        columns.append(
            jnp.sum(grads * extended[:, :, begin : begin + count].astype(jnp.float32), axis=(1, 2))
        )
    return jnp.stack(columns, axis=-1)


def shards(inputs, key_panel, value_panel, short_filters, medium_filters, lengths, cotangent):
    seqs, count, local_width = inputs.shape
    channels = key_panel.shape[1]
    groups, taps = medium_filters.shape
    group_size = channels // groups
    short_width = short_filters.shape[-1]
    span = count + taps - 1
    gathered = (
        lax.all_gather(key_panel, "dp", axis=0, tiled=True),
        lax.all_gather(value_panel, "dp", axis=0, tiled=True),
    )
    panels = jnp.concatenate([gathered[0], gathered[1]], axis=1)
    features = lax.all_gather(inputs, "shard", axis=2, tiled=True)
    projected = jnp.dot(
        features.reshape(seqs * count, -1), panels, preferred_element_type=jnp.float32
    )
    paired = projected.astype(jnp.bfloat16).reshape(seqs, count, 2, channels).transpose(2, 0, 1, 3)
    head_rows = shifted(paired[:, :, count - (short_width - 1) :], "dp", 1)
    extended = jnp.concatenate([head_rows, paired], axis=2)
    smoothed = short_taps(extended, short_filters, count)
    product = (smoothed[0] * smoothed[1]).astype(jnp.bfloat16)
    before = shifted(product[:, count - (taps - 1) :], "dp", 1)
    product_ext = jnp.concatenate([before, product], axis=1).reshape(seqs, span, groups, group_size)
    forward_band = band(medium_filters[:, ::-1], count)
    response = jnp.einsum(
        "gtr,srgm->stgm",
        forward_band,
        product_ext.astype(jnp.float32),
        precision=lax.Precision.HIGHEST,
    ).reshape(seqs, count, channels)
    position = lax.axis_index("dp") * count + jnp.arange(count, dtype=jnp.int32)
    live = (position[None, :] < lengths[:, None])[:, :, None]
    mixed = jnp.where(live, response, 0.0).astype(jnp.bfloat16)
    upstream = jnp.where(live, cotangent, jnp.zeros_like(cotangent))
    after = shifted(upstream[:, : taps - 1], "dp", -1)
    upstream_ext = jnp.concatenate([upstream, after], axis=1).reshape(
        seqs, span, groups, group_size
    )
    backward_band = band(medium_filters, count)
    product_grad = jnp.einsum(
        "gtr,srgm->stgm",
        backward_band,
        upstream_ext.astype(jnp.float32),
        precision=lax.Precision.HIGHEST,
    ).reshape(seqs, count, channels)
    correlation = jnp.einsum(
        "stgm,srgm->gtr",
        upstream.reshape(seqs, count, groups, group_size),
        product_ext,
        preferred_element_type=jnp.float32,
    )
    medium_local = band_sums(correlation, count, taps)
    smooth_grad = jnp.stack([product_grad * smoothed[1], product_grad * smoothed[0]])
    short_local = filter_terms(smooth_grad, extended, count, short_width)
    ahead_rows = shifted(smooth_grad[:, :, : short_width - 1], "dp", -1)
    pair_grad = short_ahead(
        jnp.concatenate([smooth_grad, ahead_rows], axis=2), short_filters, count
    )
    short_grad, medium_grad = lax.psum((short_local, medium_local), "dp")
    outgoing = (
        pair_grad.astype(jnp.bfloat16).transpose(1, 2, 0, 3).reshape(seqs * count, 2 * channels)
    )
    flat_features = features.reshape(seqs * count, -1)
    grads = lax.psum_scatter(
        lax.dot_general(
            flat_features, outgoing, (((0,), (0,)), ((), ())), preferred_element_type=jnp.float32
        ).astype(jnp.bfloat16),
        "dp",
        scatter_dimension=0,
        tiled=True,
    ).astype(jnp.float32)
    key_grad = grads[:, :channels].astype(jnp.bfloat16)
    value_grad = grads[:, channels:].astype(jnp.bfloat16)
    return (mixed, key_grad, value_grad, short_grad, medium_grad)


def solution(mesh):
    return jax.shard_map(
        shards,
        mesh=mesh,
        in_specs=(
            P(None, "dp", "shard"),
            P("dp", "shard"),
            P("dp", "shard"),
            P(None, "shard", None),
            P("shard", None),
            P(),
            P(None, "dp", "shard"),
        ),
        out_specs=(
            P(None, "dp", "shard"),
            P("dp", "shard"),
            P("dp", "shard"),
            P(None, "shard", None),
            P("shard", None),
        ),
        check_vma=False,
    )
```

profile of v0, /device:TPU:2, one launch (start us, length us, event | category | flops | bytes accessed | tf_op | source)
XLA Modules:
  0.0 517.8 jit_solution(16801808159717984822)
XLA Ops:
  9.4 1.0 copy.29
  11.2 7.8 %collective-permute-start.2 = (bf16[2,127,128]{1,2,0:T(8,128)(2,1)S(1)}, bf16[2,127,128]{1,2,0:T(8,128)(2,1)S(1)}, u32[]{:S(2)}, u32[]{:S(2)}) collective-permute-start(bf16[2,127,128]{1,2,0:T(8,128)(2,1)S(1)} %slice.152), channel_id=1, source_target_pairs={{32,0},{64,32},{96,64},{128,96},{160,128},{192,160},{224,192},{256... | collective-permute-start | bytes 195080 | tf_op jit(solution)/shard_map/ppermute | solution.py:10
  19.0 1.4 slice_bitcast_fusion.6
  21.3 1.9 slice.153
  23.2 5.5 %reshape.111 = f32[8,256,383,1]{2,1,0,3:T(8,128)S(1)} reshape(f32[8,98048]{1,0:T(8,128)} %slice.153) | data formatting | bytes 6275072 | tf_op jit(solution)/shard_map/reshape | solution.py:18
  29.4 79.5 %all-gather.4.cloned.1.call-done = bf16[8192,128]{1,0:T(8,128)(2,1)} async-done(((bf16[512,128]{1,0:T(8,128)(2,1)}), bf16[8192,128]{1,0:T(8,128)(2,1)}) %all-gather.4.cloned.1.call-update) | async-done | bytes 2097168 | tf_op jit(solution)/shard_map/all_gather | solution.py:66
  108.9 90.8 %all-gather.6.cloned.1.call-done = bf16[8192,128]{1,0:T(8,128)(2,1)} async-done(((bf16[512,128]{1,0:T(8,128)(2,1)}), bf16[8192,128]{1,0:T(8,128)(2,1)}) %all-gather.6.cloned.1.call-update) | async-done | bytes 2097168 | tf_op jit(solution)/shard_map/all_gather | solution.py:67
  199.8 87.3 %all-gather.8.cloned.1.call-done = bf16[2,256,8192]{2,1,0:T(8,128)(2,1)} async-done(((bf16[2,256,256]{2,1,0:T(8,128)(2,1)}), bf16[2,256,8192]{2,1,0:T(8,128)(2,1)}) %all-gather.8.cloned.1.call-update) | async-done | bytes 8388624 | tf_op jit(solution)/shard_map/all_gather | solution.py:70
  287.1 7.7 %fusion.12 = bf16[512,256]{0,1:T(8,128)(2,1)} fusion(bf16[512,8192]{1,0:T(8,128)(2,1)} %bitcast.85, bf16[8192,128]{1,0:T(8,128)(2,1)} %all-gather.6.cloned.1.call-done, bf16[8192,128]{1,0:T(8,128)(2,1)} %all-gather.4.cloned.1.call-done), kind=kOutput, calls=%fused_computation.12 | convolution fusion | flops 2156003328 | bytes 12845056 | tf_op jit(solution)/shard_map/dot_general | solution.py:71
  294.8 1.0 reshape.99
  296.0 3.4 collective-permute-start
  299.4 2.6 fusion.18
  302.1 1.5 collective-permute-done
  303.6 0.9 fusion.26
  305.3 2.1 collective-permute-start.3
  307.4 7.4 %collective-permute-done.3 = f32[2,2,6,128]{2,3,1,0:T(8,128)S(1)} collective-permute-done((f32[2,2,6,128]{2,3,1,0:T(8,128)S(1)}, f32[2,2,6,128]{2,3,1,0:T(8,128)S(1)}, u32[]{:S(2)}, u32[]{:S(2)}) %collective-permute-start.3) | collective-permute-done | bytes 12320 | tf_op jit(solution)/shard_map/ppermute | solution.py:10
  314.8 1.1 fusion.50
  316.1 7.7 %fusion = bf16[8192,256]{0,1:T(8,128)(2,1)} fusion(bf16[512,8192]{1,0:T(8,128)(2,1)} %bitcast.86, bf16[64,8,2,128]{3,2,1,0:T(2,128)(2,1)S(1)} %bitcast.93), kind=kOutput, calls=%fused_computation.1 | convolution fusion | flops 2149580800 | bytes 12845056 | tf_op jit(solution)/shard_map/dot_general | solution.py:122
  324.8 1.9 slice.151
  326.7 5.5 %reshape.110 = f32[8,256,383,1]{2,1,0,3:T(8,128)S(1)} reshape(f32[8,98048]{1,0:T(8,128)} %slice.151) | data formatting | bytes 6275072 | tf_op jit(solution)/shard_map/reshape | solution.py:18
  332.2 0.9 slice.150
  333.2 6.4 %collective-permute-start.1 = (bf16[2,127,128]{1,2,0:T(8,128)(2,1)S(1)}, bf16[2,127,128]{1,2,0:T(8,128)(2,1)S(1)}, u32[]{:S(2)}, u32[]{:S(2)}) collective-permute-start(bf16[2,127,128]{1,2,0:T(8,128)(2,1)S(1)} %slice.150), channel_id=1, source_target_pairs={{0,32},{32,64},{64,96},{96,128},{128,160},{160,192},{192,224},{224... | collective-permute-start | bytes 195080 | tf_op jit(solution)/shard_map/ppermute | solution.py:10
  339.6 3.4 fusion.32
  343.1 1.0 pad_maximum_fusion.3
  344.1 2.3 convolution_bitcast_fusion
  346.5 5.2 %reshape.108 = f32[8,98048]{1,0:T(8,128)} reshape(f32[8,256,383]{2,1,0:T(8,128)} %convolution_bitcast_fusion) | data formatting | bytes 6275072 | tf_op jit(solution)/shard_map/reshape | solution.py:23
  351.7 3.8 concatenate.31
  355.5 2.2 reduce_sum.79
  357.8 1.7 fusion.15
  360.3 118.0 %all-reduce.3 = (f32[2,128,7]{1,0,2:T(2,128)}, f32[8,128]{1,0:T(8,128)}) all-reduce(f32[2,128,7]{1,0,2:T(2,128)S(1)} %constant_dynamic-update-slice_fusion, f32[8,128]{1,0:T(8,128)S(1)} %rev.7), channel_id=1, replica_groups=mesh['dp'=16,'shard'=32] {'dp'}, use_global_device_ids=true, to_apply=%region_8.9 | all-reduce | flops 2816 | bytes 22528 | tf_op jit(solution)/shard_map/psum | solution.py:116
  478.3 30.5 %reduce-scatter.2.cloned.1.call-done = bf16[512,256]{0,1:T(8,128)(2,1)} async-done(((bf16[8192,256]{0,1:T(8,128)(2,1)}), bf16[512,256]{0,1:T(8,128)(2,1)}) %reduce-scatter.2.cloned.1.call-update) | async-done | bytes 262160 | tf_op jit(solution)/shard_map/reduce_scatter | solution.py:121
  508.8 1.0 fusion.55
  (59 shorter events, 9.1 us)
Async XLA Ops:
  7.2 101.8 %all-gather.4.cloned.1.call-start = ((), (), s32[]{:S(2)}) async-start(), calls=%async_computation.1 | async-start | bytes 2228224 | tf_op jit(solution)/shard_map/all_gather | solution.py:66
  7.9 191.9 %all-gather.6.cloned.1.call-start = ((), (), s32[]{:S(2)}) async-start(), calls=%async_computation.2 | async-start | bytes 2228224 | tf_op jit(solution)/shard_map/all_gather | solution.py:67
  8.6 278.4 %all-gather.8.cloned.1.call-start = ((), (), s32[]{:S(2)}) async-start(), calls=%async_computation.3 | async-start | bytes 8650752 | tf_op jit(solution)/shard_map/all_gather | solution.py:70
  9.4 499.4 %reduce-scatter.2.cloned.1.call-start = ((), (), s32[]{:S(2)}) async-start(), calls=%async_computation.4 | async-start | bytes 4456448 | tf_op jit(solution)/shard_map/reduce_scatter | solution.py:121
  11.2 17.5 %collective-permute-start.2 = (bf16[2,127,128]{1,2,0:T(8,128)(2,1)S(1)}, bf16[2,127,128]{1,2,0:T(8,128)(2,1)S(1)}, u32[]{:S(2)}, u32[]{:S(2)}) collective-permute-start(bf16[2,127,128]{1,2,0:T(8,128)(2,1)S(1)} %slice.152), channel_id=1, source_target_pairs={{32,0},{64,32},{96,64},{128,96},{160,128},{192,160},{224,192},{256... | collective-permute-start | bytes 195080 | tf_op jit(solution)/shard_map/ppermute | solution.py:10
  295.8 7.8 %copy-start.2 = (bf16[2,256,2,128]{1,0,3,2:T(2,128)(2,1)}, bf16[2,256,2,128]{1,0,3,2:T(2,128)(2,1)S(1)}, u32[]{:S(2)}) copy-start(bf16[2,256,2,128]{1,0,3,2:T(2,128)(2,1)S(1)} %reshape.99) | copy-start | bytes 786436
  295.8 7.7 %copy-start.5 = (f32[2,128]{1,0:T(2,128)S(1)}, f32[2,128]{1,0:T(2,128)}, u32[]{:S(2)}) copy-start(f32[2,128]{1,0:T(2,128)} %get-tuple-element.42) | copy-start | bytes 3076
  295.8 7.7 %copy-start.6 = (f32[2,128]{1,0:T(2,128)S(1)}, f32[2,128]{1,0:T(2,128)}, u32[]{:S(2)}) copy-start(f32[2,128]{1,0:T(2,128)} %get-tuple-element.43) | copy-start | bytes 3076
  295.8 7.7 %copy-start.7 = (f32[2,128]{1,0:T(2,128)S(1)}, f32[2,128]{1,0:T(2,128)}, u32[]{:S(2)}) copy-start(f32[2,128]{1,0:T(2,128)} %get-tuple-element.44) | copy-start | bytes 3076
  295.9 7.7 %copy-start.8 = (f32[2,128]{1,0:T(2,128)S(1)}, f32[2,128]{1,0:T(2,128)}, u32[]{:S(2)}) copy-start(f32[2,128]{1,0:T(2,128)} %get-tuple-element.45) | copy-start | bytes 3076
  295.9 9.3 %copy-start.1 = (bf16[2,256,2,128]{1,3,0,2:T(8,128)(2,1)}, bf16[2,256,2,128]{1,3,0,2:T(8,128)(2,1)S(1)}, u32[]{:S(2)}) copy-start(bf16[2,256,2,128]{1,3,0,2:T(8,128)(2,1)S(1)} %copy.50) | copy-start | bytes 786436
  296.0 7.5 %collective-permute-start = (bf16[2,2,6,128]{2,3,1,0:T(8,128)(2,1)S(1)}, bf16[2,2,6,128]{2,3,1,0:T(8,128)(2,1)S(1)}, u32[]{:S(2)}, u32[]{:S(2)}) collective-permute-start(bf16[2,2,6,128]{2,3,1,0:T(8,128)(2,1)S(1)} %slice.137), channel_id=1, source_target_pairs={{0,32},{32,64},{64,96},{96,128},{128,160},{160,192},{192,224},{224... | collective-permute-start | bytes 18440 | tf_op jit(solution)/shard_map/ppermute | solution.py:10
  303.6 11.2 %copy-start.3 = (bf16[2,2,6,128]{2,3,1,0:T(8,128)(2,1)}, bf16[2,2,6,128]{2,3,1,0:T(8,128)(2,1)S(1)}, u32[]{:S(2)}) copy-start(bf16[2,2,6,128]{2,3,1,0:T(8,128)(2,1)S(1)} %collective-permute-done) | copy-start | bytes 18436
  305.2 9.6 %copy-start = (f32[1,2,256,128]{2,3,1,0:T(8,128)}, f32[1,2,256,128]{2,3,1,0:T(8,128)S(1)}, u32[]{:S(2)}) copy-start(f32[1,2,256,128]{2,3,1,0:T(8,128)S(1)} %get-tuple-element.35) | copy-start | bytes 786436
  305.3 9.5 %collective-permute-start.3 = (f32[2,2,6,128]{2,3,1,0:T(8,128)S(1)}, f32[2,2,6,128]{2,3,1,0:T(8,128)S(1)}, u32[]{:S(2)}, u32[]{:S(2)}) collective-permute-start(f32[2,2,6,128]{2,3,1,0:T(8,128)S(1)} %fusion.46), channel_id=1, source_target_pairs={{32,0},{64,32},{96,64},{128,96},{160,128},{192,160},{224,192},{256... | collective-permute-start | bytes 36872 | tf_op jit(solution)/shard_map/ppermute | solution.py:10
  323.8 0.7 copy-start.4
  333.2 9.9 %collective-permute-start.1 = (bf16[2,127,128]{1,2,0:T(8,128)(2,1)S(1)}, bf16[2,127,128]{1,2,0:T(8,128)(2,1)S(1)}, u32[]{:S(2)}, u32[]{:S(2)}) collective-permute-start(bf16[2,127,128]{1,2,0:T(8,128)(2,1)S(1)} %slice.150), channel_id=1, source_target_pairs={{0,32},{32,64},{64,96},{96,128},{128,160},{160,192},{192,224},{224... | collective-permute-start | bytes 195080 | tf_op jit(solution)/shard_map/ppermute | solution.py:10
Sparse Core Ops, SparseCore 0:
  11.0 97.9 all-gather.3
  111.9 87.7 all-gather.5
  201.8 85.1 all-gather.7
  324.0 184.7 reduce-scatter.1
where the time goes:
time: 519 us; the launch traced here: 518 us
  waiting for transfers between devices  299 us (58%)
  blocking collectives  118 us (23%)
  local copies, waits for them, and re-layouts  33.8 us (7%)
  matrix products  22.1 us (4%)
  starting transfers between devices  19.8 us (4%)
  between operations  14.1 us (3%)
  other arithmetic  10.9 us (2%)
    psum x1, blocking collectives, shards(): short_grad, medium_grad = lax.psum((short_local, medium_local), 'dp')  118 us
    all_gather x1, waiting for transfers between devices, shards(): lax.all_gather(value_panel, 'dp', axis=0, tiled=True)  90.8 us
    all_gather x1, waiting for transfers between devices, shards(): features = lax.all_gather(inputs, 'shard', axis=2, tiled=True)  87.3 us
    all_gather x1, waiting for transfers between devices, shards(): lax.all_gather(key_panel, 'dp', axis=0, tiled=True)  79.5 us
    reduce_scatter x1, waiting for transfers between devices, shards(): lax.psum_scatter(lax.dot_general(flat_features, outgoing, (((0,), (0,)),...  30.5 us
    ppermute x4, starting transfers between devices, shifted(): lax.ppermute(value, axis, [(source, source + steps) for source in range(f...  19.7 us
    reshape x2, local copies, waits for them, and re-layouts, band(): return tiled.reshape(groups, count, width)  11.1 us
  transfers between devices with their start and end apart: 8, of which 6 were waited for; matrix products, arithmetic and copies ran while one was open for 8% of the time, Pallas kernels for 0%

commit v1 on v0

--- a/solution.py
+++ b/solution.py
@@ -67,7 +67,9 @@
         lax.all_gather(value_panel, "dp", axis=0, tiled=True),
     )
     panels = jnp.concatenate([gathered[0], gathered[1]], axis=1)
-    features = lax.all_gather(inputs, "shard", axis=2, tiled=True)
+    features = jnp.concatenate(
+        lax.all_to_all(jnp.stack([inputs] * lax.axis_size("shard")), "shard", 0, 0), axis=2
+    )
     projected = jnp.dot(
         features.reshape(seqs * count, -1), panels, preferred_element_type=jnp.float32
     )

time: 519 us -> 559 us (1.077)
  the two profiles are of different devices: /device:TPU:2 before, /device:TPU:24 now
where the time goes in v1:
time: 559 us; the launch traced here: 549 us
  waiting for transfers between devices  297 us (53%)
  blocking collectives  122 us (22%)
  local copies, waits for them, and re-layouts  64.1 us (11%)
  matrix products  22 us (4%)
  starting transfers between devices  18.6 us (3%)
  between operations  14.4 us (3%)
  other arithmetic  10.3 us (2%)
    all_to_all x1, waiting for transfers between devices, shards(): lax.all_to_all(jnp.stack([inputs] * lax.axis_size('shard')), 'shard', 0, 0)  258 us
    psum x1, blocking collectives, shards(): short_grad, medium_grad = lax.psum((short_local, medium_local), 'dp')  122 us
    reduce_scatter x1, waiting for transfers between devices, shards(): lax.psum_scatter(lax.dot_general(flat_features, outgoing, (((0,), (0,)),...  28.6 us
    unnamed x37, local copies, waits for them, and re-layouts  19.4 us
    reshape x1, local copies, waits for them, and re-layouts, shards(): jnp.concatenate(lax.all_to_all(jnp.stack([inputs] * lax.axis_size('shard'...  11.4 us
  transfers between devices with their start and end apart: 8, of which 4 were waited for; matrix products, arithmetic and copies ran while one was open for 13% of the time, Pallas kernels for 0%

profile of v1, /device:TPU:24, one launch (start us, length us, event | category | flops | bytes accessed | tf_op | source)
XLA Modules:
  0.0 549.0 jit_solution(17187743497083070151)
XLA Ops:
  7.2 5.2 stack.20
  12.4 10.4 %all-to-all-start = ((bf16[32,2,256,256]{3,2,1,0:T(8,128)(2,1)}), bf16[32,2,256,256]{3,2,1,0:T(8,128)(2,1)}, u32[]{:S(2)}, u32[]{:S(2)}) async-start(bf16[32,2,256,256]{3,2,1,0:T(8,128)(2,1)} %stack.20), calls=%async_computation | async-start | bytes 16777216 | tf_op jit(solution)/shard_map/all_to_all | solution.py:71
  24.6 1.3 collective-permute-start.2
  26.7 1.8 slice.153
  28.5 5.5 %reshape.112 = f32[8,256,383,1]{2,1,0,3:T(8,128)S(1)} reshape(f32[8,98048]{1,0:T(8,128)} %slice.153) | data formatting | bytes 6275072 | tf_op jit(solution)/shard_map/reshape | solution.py:18
  34.8 258.1 %all-to-all-done = bf16[32,2,256,256]{3,2,1,0:T(8,128)(2,1)} async-done(((bf16[32,2,256,256]{3,2,1,0:T(8,128)(2,1)}), bf16[32,2,256,256]{3,2,1,0:T(8,128)(2,1)}, u32[]{:S(2)}, u32[]{:S(2)}) %all-to-all-start) | async-done | bytes 8388640 | tf_op jit(solution)/shard_map/all_to_all | solution.py:71
  292.8 11.4 %copy.36 = bf16[2,256,32,256]{3,2,1,0:T(8,128)(2,1)} copy(bf16[2,256,32,256]{3,1,0,2:T(8,128)(2,1)} %bitcast.1) | data formatting | bytes 16777216 | tf_op jit(solution)/shard_map/reshape | solution.py:70
  304.2 16.9 %copy.49 = bf16[64,8,32,256]{3,1,2,0:T(8,128)(2,1)} copy(bf16[64,8,32,256]{3,2,1,0:T(8,128)(2,1)} %bitcast.87) | data formatting | bytes 16777216
  321.1 7.8 %fusion.12 = bf16[512,256]{0,1:T(8,128)(2,1)} fusion(bf16[512,8192]{1,0:T(8,128)(2,1)} %bitcast.85, bf16[8192,128]{1,0:T(8,128)(2,1)} %all-gather.5.cloned.1.call-done, bf16[8192,128]{1,0:T(8,128)(2,1)} %all-gather.3.cloned.1.call-done), kind=kOutput, calls=%fused_computation.12 | convolution fusion | flops 2156003328 | bytes 12845056 | tf_op jit(solution)/shard_map/dot_general | solution.py:73
  328.9 1.0 reshape.100
  330.1 1.6 collective-permute-start
  331.7 2.6 fusion.18
  334.8 0.9 fusion.26
  336.4 1.3 collective-permute-start.3
  337.7 9.0 %collective-permute-done.3 = f32[2,2,6,128]{2,3,1,0:T(8,128)S(1)} collective-permute-done((f32[2,2,6,128]{2,3,1,0:T(8,128)S(1)}, f32[2,2,6,128]{2,3,1,0:T(8,128)S(1)}, u32[]{:S(2)}, u32[]{:S(2)}) %collective-permute-start.3) | collective-permute-done | bytes 12320 | tf_op jit(solution)/shard_map/ppermute | solution.py:10
  346.8 1.1 fusion.50
  348.1 7.7 %fusion = bf16[8192,256]{0,1:T(8,128)(2,1)} fusion(bf16[512,8192]{1,0:T(8,128)(2,1)} %bitcast.86, bf16[64,8,2,128]{3,2,1,0:T(2,128)(2,1)S(1)} %bitcast.97), kind=kOutput, calls=%fused_computation.1 | convolution fusion | flops 2149580800 | bytes 12845056 | tf_op jit(solution)/shard_map/dot_general | solution.py:124
  356.1 1.8 slice.151
  358.0 5.5 %reshape.111 = f32[8,256,383,1]{2,1,0,3:T(8,128)S(1)} reshape(f32[8,98048]{1,0:T(8,128)} %slice.151) | data formatting | bytes 6275072 | tf_op jit(solution)/shard_map/reshape | solution.py:18
  363.5 0.9 slice.150
  364.4 3.9 collective-permute-start.1
  368.3 3.4 fusion.32
  371.8 1.0 pad_maximum_fusion.3
  372.9 2.3 convolution_bitcast_fusion
  375.1 5.2 reshape.109
  380.4 3.7 concatenate.31
  384.1 2.2 reduce_sum.79
  386.4 1.7 fusion.15
  388.1 0.8 copy.44
  388.9 122.2 %all-reduce.3 = (f32[2,128,7]{1,0,2:T(2,128)}, f32[8,128]{1,0:T(8,128)}) all-reduce(f32[2,128,7]{1,0,2:T(2,128)S(1)} %constant_dynamic-update-slice_fusion, f32[8,128]{1,0:T(8,128)S(1)} %rev.7), channel_id=1, replica_groups=mesh['dp'=16,'shard'=32] {'dp'}, use_global_device_ids=true, to_apply=%region_8.9 | all-reduce | flops 2816 | bytes 22528 | tf_op jit(solution)/shard_map/psum | solution.py:118
  511.1 28.6 %reduce-scatter.2.cloned.1.call-done = bf16[512,256]{0,1:T(8,128)(2,1)} async-done(((bf16[8192,256]{0,1:T(8,128)(2,1)}), bf16[512,256]{0,1:T(8,128)(2,1)}) %reduce-scatter.2.cloned.1.call-update) | async-done | bytes 262160 | tf_op jit(solution)/shard_map/reduce_scatter | solution.py:123
  539.7 1.0 fusion.55
  (69 shorter events, 6.7 us)
Async XLA Ops:
  12.4 12.0 %copy-start.4 = (bf16[2,256,128]{2,1,0:T(8,128)(2,1)S(1)}, bf16[2,256,128]{2,1,0:T(8,128)(2,1)}, u32[]{:S(2)}) copy-start(bf16[2,256,128]{2,1,0:T(8,128)(2,1)} %param.13) | copy-start | bytes 393220
  12.4 12.1 %copy-start.12 = (s32[2]{0:T(128)S(1)}, s32[2]{0:T(128)}, u32[]{:S(2)}) copy-start(s32[2]{0:T(128)} %param.12) | copy-start | bytes 28
  12.4 13.5 %copy-start.11 = (f32[2,128,7]{1,0,2:T(2,128)S(1)}, f32[2,128,7]{1,0,2:T(2,128)}, u32[]{:S(2)}) copy-start(f32[2,128,7]{1,0,2:T(2,128)} %param.10) | copy-start | bytes 21508
  12.4 14.1 %copy-start.5 = (f32[8,128]{1,0:T(8,128)S(1)}, f32[8,128]{1,0:T(8,128)}, u32[]{:S(2)}) copy-start(f32[8,128]{1,0:T(8,128)} %param.11) | copy-start | bytes 12292
  12.4 280.5 %all-to-all-start = ((bf16[32,2,256,256]{3,2,1,0:T(8,128)(2,1)}), bf16[32,2,256,256]{3,2,1,0:T(8,128)(2,1)}, u32[]{:S(2)}, u32[]{:S(2)}) async-start(bf16[32,2,256,256]{3,2,1,0:T(8,128)(2,1)} %stack.20), calls=%async_computation | async-start | bytes 16777216 | tf_op jit(solution)/shard_map/all_to_all | solution.py:71
  22.8 298.3 %all-gather.3.cloned.1.call-start = ((), (), s32[]{:S(2)}) async-start(), calls=%async_computation.2 | async-start | bytes 2228224 | tf_op jit(solution)/shard_map/all_gather | solution.py:66
  23.5 297.6 %all-gather.5.cloned.1.call-start = ((), (), s32[]{:S(2)}) async-start(), calls=%async_computation.3 | async-start | bytes 2228224 | tf_op jit(solution)/shard_map/all_gather | solution.py:67
  24.3 515.4 %reduce-scatter.2.cloned.1.call-start = ((), (), s32[]{:S(2)}) async-start(), calls=%async_computation.4 | async-start | bytes 4456448 | tf_op jit(solution)/shard_map/reduce_scatter | solution.py:123
  24.6 9.5 %collective-permute-start.2 = (bf16[2,127,128]{1,2,0:T(8,128)(2,1)S(1)}, bf16[2,127,128]{1,2,0:T(8,128)(2,1)S(1)}, u32[]{:S(2)}, u32[]{:S(2)}) collective-permute-start(bf16[2,127,128]{1,2,0:T(8,128)(2,1)S(1)} %slice.152), channel_id=1, source_target_pairs={{32,0},{64,32},{96,64},{128,96},{160,128},{192,160},{224,192},{256... | collective-permute-start | bytes 195080 | tf_op jit(solution)/shard_map/ppermute | solution.py:10
  329.9 4.8 copy-start.2
  329.9 4.8 copy-start.6
  329.9 4.8 copy-start.7
  329.9 4.8 copy-start.8
  329.9 4.8 copy-start.9
  330.0 4.8 copy-start.10
  330.0 6.4 %copy-start.1 = (bf16[2,256,2,128]{1,3,0,2:T(8,128)(2,1)}, bf16[2,256,2,128]{1,3,0,2:T(8,128)(2,1)S(1)}, u32[]{:S(2)}) copy-start(bf16[2,256,2,128]{1,3,0,2:T(8,128)(2,1)S(1)} %copy.62) | copy-start | bytes 786436
  330.1 4.6 collective-permute-start
  334.7 12.0 %copy-start.3 = (bf16[2,2,6,128]{2,3,1,0:T(8,128)(2,1)}, bf16[2,2,6,128]{2,3,1,0:T(8,128)(2,1)S(1)}, u32[]{:S(2)}) copy-start(bf16[2,2,6,128]{2,3,1,0:T(8,128)(2,1)S(1)} %collective-permute-done) | copy-start | bytes 18436
  336.4 10.4 %copy-start = (f32[1,2,256,128]{2,3,1,0:T(8,128)}, f32[1,2,256,128]{2,3,1,0:T(8,128)S(1)}, u32[]{:S(2)}) copy-start(f32[1,2,256,128]{2,3,1,0:T(8,128)S(1)} %get-tuple-element.40) | copy-start | bytes 786436
  336.4 10.3 %collective-permute-start.3 = (f32[2,2,6,128]{2,3,1,0:T(8,128)S(1)}, f32[2,2,6,128]{2,3,1,0:T(8,128)S(1)}, u32[]{:S(2)}, u32[]{:S(2)}) collective-permute-start(f32[2,2,6,128]{2,3,1,0:T(8,128)S(1)} %fusion.46), channel_id=1, source_target_pairs={{32,0},{64,32},{96,64},{128,96},{160,128},{192,160},{224,192},{256... | collective-permute-start | bytes 36872 | tf_op jit(solution)/shard_map/ppermute | solution.py:10
  364.4 7.4 %collective-permute-start.1 = (bf16[2,127,128]{1,2,0:T(8,128)(2,1)S(1)}, bf16[2,127,128]{1,2,0:T(8,128)(2,1)S(1)}, u32[]{:S(2)}, u32[]{:S(2)}) collective-permute-start(bf16[2,127,128]{1,2,0:T(8,128)(2,1)S(1)} %slice.150), channel_id=1, source_target_pairs={{0,32},{32,64},{64,96},{96,128},{128,160},{160,192},{192,224},{224... | collective-permute-start | bytes 195080 | tf_op jit(solution)/shard_map/ppermute | solution.py:10
Sparse Core Ops, SparseCore 0:
  26.6 99.5 all-gather.2
  129.2 129.6 all-gather.4
  355.9 183.7 reduce-scatter.1
